TPU v7x, 512 devices: a whole 4x8x8 slice. The times are simulated.
512 devices in a mesh: occ: 64 (over x, y, core), aux: 8 (over z).
Axes of the slice: x: 4, y: 8, z: 8, core: 2. Of those that a mesh axis runs over, the one named last changes fastest.
Arguments:
- ao_blocks: bfloat16 [256, 256, 8192], P('occ', None, 'aux'), may hold values from -0.59765625 to 0.59765625
- pno_coef: bfloat16 [1024, 256, 200], P('occ'), may hold values from -0.375 to 0.375
- pno_energy: float32 [1024, 200], P('occ'), may hold values from 0.3 to 3
- occ_energy: float32 [256], replicated, may hold values from -1.5 to -0.3
- pair_partner: int32 [1024], P('occ'), may hold values from 0 to 255, as said below
- pno_count: int32 [1024], P('occ'), may hold values from 40 to 200, as said below
Outputs:
- amplitudes: float32 [1024, 200, 200], P(('occ', 'aux'))
- orbital_pair_energy: float32 [256], P('occ')
Inputs may be any that keep to these rules, and one draw needn't show every extreme that they name: pair_partner[s] differs from own(s) and is an orbital owned by the same index of occ as own(s), or by the index just below or just above it. `pno_count`: every count is a multiple of 8; in every block of 16 pairs one count is 200 and one is 40.
All inputs are finite; a program needn't handle non-finite values.
Results may differ from a plain program's by a relative error of at most 0.0041.
Values may be sent and summed in bfloat16 or wider, within the bound.
A program may use at most 128 MiB of HBM per device.

v0:
```python
import jax
import jax.numpy as jnp
from jax import lax
from jax.sharding import PartitionSpec as P


def padded(cells, sides, width):
    for axis, dim in sides:
        count = lax.axis_size(axis)
        ends = count - 1
        head = lax.slice_in_dim(cells, 0, width, axis=dim)
        tail = lax.slice_in_dim(cells, cells.shape[dim] - width, cells.shape[dim], axis=dim)
        cells = jnp.concatenate(
            [
                lax.ppermute(tail, axis, [(i, (i + 1) % count) for i in range(ends)]),
                cells,
                lax.ppermute(head, axis, [((i + 1) % count, i) for i in range(ends)]),
            ],
            axis=dim,
        )
    return cells


def shards(ao_blocks, pno_coef, pno_energy, occ_energy, pair_partner, pno_count):
    orb_dev = ao_blocks.shape[0]
    virtuals = ao_blocks.shape[1]
    aux_block = ao_blocks.shape[2]
    pair_dev = pno_coef.shape[0]
    pno_max = pno_coef.shape[2]
    per_orbital = pair_dev // orb_dev
    occ_place = lax.axis_index("occ")
    aux_place = lax.axis_index("aux")
    columns = jnp.arange(pno_max, dtype=jnp.int32)
    kept_mask = (columns[None, :] < pno_count[:, None]).astype(jnp.bfloat16)
    masked_coef = pno_coef * kept_mask[:, None, :]
    projected_own = (
        jnp.einsum(
            "ornp,onk->orpk",
            masked_coef.reshape(orb_dev, per_orbital, virtuals, pno_max),
            ao_blocks,
            preferred_element_type=jnp.float32,
        )
        .astype(jnp.bfloat16)
        .reshape(pair_dev, pno_max, aux_block)
    )
    nearby = padded(ao_blocks, (("occ", 0),), orb_dev)
    window_slot = pair_partner - (occ_place - 1) * orb_dev
    partner_blocks = jnp.take(nearby, window_slot, axis=0)
    projected_partner = jnp.einsum(
        "snp,snk->spk", masked_coef, partner_blocks, preferred_element_type=jnp.float32
    ).astype(jnp.bfloat16)
    partials = jnp.einsum(
        "spk,sqk->spq", projected_own, projected_partner, preferred_element_type=jnp.float32
    )
    share_rows = pair_dev // lax.axis_size("aux")
    first_row = aux_place * share_rows
    totals = lax.psum(partials, "aux")
    exchange_ints = lax.dynamic_slice_in_dim(totals, first_row, share_rows, 0)
    own_orbital = occ_place * orb_dev + jnp.arange(pair_dev, dtype=jnp.int32) // per_orbital
    mine_owner = lax.dynamic_slice_in_dim(own_orbital, first_row, share_rows, 0)
    mine_partner = lax.dynamic_slice_in_dim(pair_partner, first_row, share_rows, 0)
    energies = lax.dynamic_slice_in_dim(pno_energy, first_row, share_rows, 0)
    shift_occ = occ_energy[mine_owner] + occ_energy[mine_partner]
    denominator = energies[:, :, None] + energies[:, None, :] - shift_occ[:, None, None]
    amplitudes = -exchange_ints / denominator
    pair_energy = jnp.sum(
        (2.0 * exchange_ints - jnp.swapaxes(exchange_ints, 1, 2)) * amplitudes, axis=(1, 2)
    )
    half_energy = 0.5 * pair_energy
    orbital_ids = jnp.arange(occ_energy.shape[0], dtype=jnp.int32)
    hits = (orbital_ids[None, :] == mine_owner[:, None]).astype(jnp.float32) + (
        orbital_ids[None, :] == mine_partner[:, None]
    ).astype(jnp.float32)
    spread = jnp.sum(hits * half_energy[:, None], axis=0)
    whole_sum = lax.psum(spread, ("occ", "aux"))
    orbital = lax.dynamic_slice_in_dim(whole_sum, occ_place * orb_dev, orb_dev, 0)
    return (amplitudes, orbital)


def solution(mesh):
    return jax.shard_map(
        shards,
        mesh=mesh,
        in_specs=(
            P("occ", None, "aux"),
            P("occ", None, None),
            P("occ", None),
            P(),
            P("occ"),
            P("occ"),
        ),
        out_specs=(P(("occ", "aux"), None, None), P("occ")),
        check_vma=False,
    )
```

profile of v0, /device:TPU:1, one launch (start us, length us, event | category | flops | bytes accessed | tf_op | source)
XLA Modules:
  0.0 275.3 jit_solution(15171100014383080903)
XLA Ops:
  7.2 0.0 copy-start
  7.2 0.0 copy-start.2
  7.2 0.0 all-reduce.2.cloned.1.call-start
  7.2 4.7 %collective-permute-start = (bf16[4,256,1024]{2,1,0:T(8,128)(2,1)}, bf16[4,256,1024]{2,1,0:T(8,128)(2,1)}, u32[]{:S(2)}, u32[]{:S(2)}) collective-permute-start(bf16[4,256,1024]{2,1,0:T(8,128)(2,1)} %param.6), channel_id=1, source_target_pairs={{0,8},{8,16},{16,24},{24,32},{32,40},{40,48},{48,56},{56,64},{64,7... | collective-permute-start | bytes 6291464 | tf_op jit(solution)/shard_map/ppermute | solution.py:15
  12.0 6.8 %collective-permute-start.1 = (bf16[4,256,1024]{2,1,0:T(8,128)(2,1)}, bf16[4,256,1024]{2,1,0:T(8,128)(2,1)}, u32[]{:S(2)}, u32[]{:S(2)}) collective-permute-start(bf16[4,256,1024]{2,1,0:T(8,128)(2,1)} %param.6), channel_id=1, source_target_pairs={{8,0},{16,8},{24,16},{32,24},{40,32},{48,40},{56,48},{64,56},{72,6... | collective-permute-start | bytes 6291464 | tf_op jit(solution)/shard_map/ppermute | solution.py:17
  18.7 0.7 compare_and_fusion
  19.4 0.7 fusion.13
  20.1 1.9 broadcast_multiply_fusion
  22.0 0.0 copy-start.3
  22.1 0.0 copy-done.2
  22.1 4.7 %convolution_convert_fusion = bf16[4,4,200,1024]{3,2,1,0:T(8,128)(2,1)} fusion(bf16[4,4,256,200]{2,3,1,0:T(8,128)(2,1)S(1)} %bitcast.16, bf16[4,256,1024]{2,1,0:T(8,128)(2,1)S(1)} %copy-done.2), kind=kOutput, calls=%fused_computation.8 | convolution fusion | flops 1680998400 | bytes 10289152 | tf_op jit(solution)/shard_map/ornp,onk->orpk/dot_general | solution.py:37
  26.8 0.0 copy-done.3
  26.8 8.5 %collective-permute-done = bf16[4,256,1024]{2,1,0:T(8,128)(2,1)} collective-permute-done((bf16[4,256,1024]{2,1,0:T(8,128)(2,1)}, bf16[4,256,1024]{2,1,0:T(8,128)(2,1)}, u32[]{:S(2)}, u32[]{:S(2)}) %collective-permute-start) | collective-permute-done | bytes 2097184 | tf_op jit(solution)/shard_map/ppermute | solution.py:15
  35.2 4.4 %collective-permute-done.1 = bf16[4,256,1024]{2,1,0:T(8,128)(2,1)} collective-permute-done((bf16[4,256,1024]{2,1,0:T(8,128)(2,1)}, bf16[4,256,1024]{2,1,0:T(8,128)(2,1)}, u32[]{:S(2)}, u32[]{:S(2)}) %collective-permute-start.1) | collective-permute-done | bytes 2097184 | tf_op jit(solution)/shard_map/ppermute | solution.py:17
  39.6 5.5 %pad_maximum_fusion = bf16[12,256,1024]{2,1,0:T(8,128)(2,1)} fusion(bf16[4,256,1024]{2,1,0:T(8,128)(2,1)} %collective-permute-done.1, bf16[4,256,1024]{2,1,0:T(8,128)(2,1)S(1)} %copy-done.2, bf16[4,256,1024]{2,1,0:T(8,128)(2,1)} %collective-permute-done), kind=kLoop, calls=%fused_computation.7 | loop fusion | flops 6291456 | bytes 12582912 | tf_op jit(solution)/shard_map/concatenate | solution.py:13
  45.1 7.7 %gather_fusion = bf16[16,256,1024]{2,1,0:T(8,128)(2,1)} fusion(bf16[12,256,1024]{2,1,0:T(8,128)(2,1)} %pad_maximum_fusion, s32[1024]{0:T(1024)S(1)} %pad_clamp_fusion.2), kind=kCustom, calls=%fused_computation | custom fusion | bytes 16777280 | tf_op jit(solution)/shard_map/jit(_take)/gather | solution.py:48
  52.8 0.0 copy-done.4
  52.8 10.8 %fusion.9 = f32[16,200,200]{2,1,0:T(8,128)} fusion(bf16[16,200,1024]{2,1,0:T(8,128)(2,1)} %bitcast.17, bf16[16,256,200]{1,2,0:T(8,128)(2,1)S(1)} %copy-done.4, bf16[16,256,1024]{2,1,0:T(8,128)(2,1)} %gather_fusion, pred[16]{0:T(512)(128)(4,1)S(1)} %get-tuple-element.12), kind=kOutput, calls=%fused_computation.11 | convolution fusion | flops 2995912704 | bytes 19140624 | tf_op jit(solution)/shard_map/spk,sqk->spq/dot_general | solution.py:52
  63.6 0.0 all-reduce.2.cloned.1.call-update
  63.6 0.0 copy-done.5
  63.6 0.1 compare_select_fusion
  63.7 0.0 copy-done.1
  63.7 0.6 gather_fusion.1
  64.3 0.6 gather_fusion.2
  65.0 102.3 %all-reduce.2.cloned.1.call-done = f32[16,200,200]{2,1,0:T(8,128)} async-done(((f32[16,200,200]{2,1,0:T(8,128)}), f32[16,200,200]{2,1,0:T(8,128)}) %all-reduce.2.cloned.1.call-update) | async-done | bytes 2560016 | tf_op jit(solution)/shard_map/psum | solution.py:57
  167.3 1.0 constant_dynamic-slice_fusion.1
  168.3 0.2 copy.14
  168.5 1.3 fusion.12
  169.8 0.9 copy.16
  170.8 0.1 fusion.16
  170.8 97.1 %psum.15 = f32[256]{0:T(256)S(1)} all-reduce(f32[256]{0:T(256)S(1)} %fusion.16), channel_id=1, replica_groups=mesh['occ'=64,'aux'=8] {'occ','aux'}, use_global_device_ids=true, to_apply=%region_3.4 | all-reduce | flops 256 | bytes 2048 | tf_op jit(solution)/shard_map/psum | solution.py:75
  267.9 0.6 dynamic_slice.19
  (11 shorter events, 0.0 us)
Async XLA Ops:
  7.2 57.8 %copy-start = (f32[16,200]{1,0:T(8,128)S(1)}, f32[16,200]{1,0:T(8,128)}, u32[]{:S(2)}) copy-start(f32[16,200]{1,0:T(8,128)} %param.8) | copy-start | bytes 38404
  7.2 14.9 %copy-start.2 = (bf16[4,256,1024]{2,1,0:T(8,128)(2,1)S(1)}, bf16[4,256,1024]{2,1,0:T(8,128)(2,1)}, u32[]{:S(2)}) copy-start(bf16[4,256,1024]{2,1,0:T(8,128)(2,1)} %param.6) | copy-start | bytes 6291460
  7.2 160.1 %all-reduce.2.cloned.1.call-start = ((), (), s32[]{:S(2)}) async-start(), calls=%async_computation | async-start | bytes 6553600 | tf_op jit(solution)/shard_map/psum | solution.py:57
  7.2 28.0 %collective-permute-start = (bf16[4,256,1024]{2,1,0:T(8,128)(2,1)}, bf16[4,256,1024]{2,1,0:T(8,128)(2,1)}, u32[]{:S(2)}, u32[]{:S(2)}) collective-permute-start(bf16[4,256,1024]{2,1,0:T(8,128)(2,1)} %param.6), channel_id=1, source_target_pairs={{0,8},{8,16},{16,24},{24,32},{32,40},{40,48},{48,56},{56,64},{64,7... | collective-permute-start | bytes 6291464 | tf_op jit(solution)/shard_map/ppermute | solution.py:15
  12.0 27.7 %collective-permute-start.1 = (bf16[4,256,1024]{2,1,0:T(8,128)(2,1)}, bf16[4,256,1024]{2,1,0:T(8,128)(2,1)}, u32[]{:S(2)}, u32[]{:S(2)}) collective-permute-start(bf16[4,256,1024]{2,1,0:T(8,128)(2,1)} %param.6), channel_id=1, source_target_pairs={{8,0},{16,8},{24,16},{32,24},{40,32},{48,40},{56,48},{64,56},{72,6... | collective-permute-start | bytes 6291464 | tf_op jit(solution)/shard_map/ppermute | solution.py:17
  22.0 4.7 %copy-start.3 = (bf16[16,256,200]{1,2,0:T(8,128)(2,1)}, bf16[16,256,200]{1,2,0:T(8,128)(2,1)S(1)}, u32[]{:S(2)}) copy-start(bf16[16,256,200]{1,2,0:T(8,128)(2,1)S(1)} %broadcast_multiply_fusion) | copy-start | bytes 4915204
  45.1 7.7 %copy-start.4 = (bf16[16,256,200]{1,2,0:T(8,128)(2,1)S(1)}, bf16[16,256,200]{1,2,0:T(8,128)(2,1)}, u32[]{:S(2)}) copy-start(bf16[16,256,200]{1,2,0:T(8,128)(2,1)} %copy-done.3) | copy-start | bytes 4915204
  52.8 10.8 %copy-start.5 = (s32[16]{0:T(128)S(1)}, s32[16]{0:T(128)}, u32[]{:S(2)}) copy-start(s32[16]{0:T(128)} %param.10) | copy-start | bytes 196
  52.8 10.9 %copy-start.1 = (f32[256]{0:T(256)S(1)}, f32[256]{0:T(256)}, u32[]{:S(2)}) copy-start(f32[256]{0:T(256)} %param.9) | copy-start | bytes 3076
Sparse Core Ops, SparseCore 0:
  63.7 103.5 all-reduce.1
where the time goes:
time: 276 us; the launch traced here: 275 us
  waiting for transfers between devices  115 us (42%)
  blocking collectives  97.1 us (35%)
  matrix products  15.4 us (6%)
  between operations  14.1 us (5%)
  local copies, waits for them, and re-layouts  11.7 us (4%)
  starting transfers between devices  11.5 us (4%)
  other arithmetic  10.3 us (4%)
    psum x1, waiting for transfers between devices, shards(): totals = lax.psum(partials, 'aux')  102 us
    psum x1, blocking collectives, shards(): whole_sum = lax.psum(spread, ('occ', 'aux'))  97.1 us
    dot_general x1, matrix products, shards(): jnp.einsum('spk,sqk->spq', projected_own, projected_partner, preferred_el...  10.8 us
    ppermute x1, waiting for transfers between devices, padded(): lax.ppermute(tail, axis, [(i, (i + 1) % count) for i in range(ends)])  8.47 us
    gather x1, local copies, waits for them, and re-layouts, shards(): partner_blocks = jnp.take(nearby, window_slot, axis=0)  7.67 us
    ppermute x1, starting transfers between devices, padded(): lax.ppermute(head, axis, [((i + 1) % count, i) for i in range(ends)])  6.75 us
  transfers between devices with their start and end apart: 3, of which 3 were waited for; matrix products, arithmetic and copies ran while one was open for 3% of the time, Pallas kernels for 0%

commit v1 on v0

--- a/solution.py
+++ b/solution.py
@@ -54,7 +54,9 @@
     )
     share_rows = pair_dev // lax.axis_size("aux")
     first_row = aux_place * share_rows
-    totals = lax.psum(partials, "aux")
+    totals = partials
+    for hop in (1, 2, 4):
+        totals = totals + lax.ppermute(totals, "aux", [(dev, dev ^ hop) for dev in range(8)])
     exchange_ints = lax.dynamic_slice_in_dim(totals, first_row, share_rows, 0)
     own_orbital = occ_place * orb_dev + jnp.arange(pair_dev, dtype=jnp.int32) // per_orbital
     mine_owner = lax.dynamic_slice_in_dim(own_orbital, first_row, share_rows, 0)

time: 276 us -> 572 us (2.07)
  waiting for transfers between devices: 115 us -> 414 us
  between operations: 14.1 us -> 0.79 us
  starting transfers between devices: 11.5 us -> 21.4 us
    ppermute x0 -> x3, waiting for transfers between devices: none -> 401 us  [shards(): lax.ppermute(totals, 'aux', [(dev, dev ^ hop) for dev in range(8)])]
    psum x1 -> x0, waiting for transfers between devices: 102 us -> none  [shards(): totals = lax.psum(partials, 'aux')]
    ppermute x0 -> x3, starting transfers between devices: none -> 9.95 us  [shards(): lax.ppermute(totals, 'aux', [(dev, dev ^ hop) for dev in range(8)])]
  transfers between devices with their start and end apart: 3 -> 5, of which waited for: 3 -> 5; matrix products, arithmetic and copies ran while one was open for 3% -> 2% of each run, Pallas kernels for 0% -> 0%
where the time goes in v1:
time: 572 us; the launch traced here: 571 us
  waiting for transfers between devices  414 us (72%)
  blocking collectives  93.2 us (16%)
  starting transfers between devices  21.4 us (4%)
  matrix products  15.4 us (3%)
  other arithmetic  14.9 us (3%)
  local copies, waits for them, and re-layouts  11.7 us (2%)
    ppermute x3, waiting for transfers between devices, shards(): lax.ppermute(totals, 'aux', [(dev, dev ^ hop) for dev in range(8)])  401 us
    psum x1, blocking collectives, shards(): whole_sum = lax.psum(spread, ('occ', 'aux'))  93.2 us
  transfers between devices with their start and end apart: 5, of which 5 were waited for; matrix products, arithmetic and copies ran while one was open for 2% of the time, Pallas kernels for 0%

profile of v1, /device:TPU:1, one launch (start us, length us, event | category | flops | bytes accessed | tf_op | source)
XLA Modules:
  0.0 571.2 jit_solution(9641644705544006679)
XLA Ops:
  0.6 0.0 copy-start
  0.7 4.7 collective-permute-start
  5.4 6.7 %collective-permute-start.1 = (bf16[4,256,1024]{2,1,0:T(8,128)(2,1)}, bf16[4,256,1024]{2,1,0:T(8,128)(2,1)}, u32[]{:S(2)}, u32[]{:S(2)}) collective-permute-start(bf16[4,256,1024]{2,1,0:T(8,128)(2,1)} %param.6), channel_id=1, source_target_pairs={{8,0},{16,8},{24,16},{32,24},{40,32},{48,40},{56,48},{64,56},{72,6... | collective-permute-start | bytes 6291464 | tf_op jit(solution)/shard_map/ppermute | solution.py:17
  12.1 0.7 compare_and_fusion
  12.8 0.7 fusion.13
  13.5 1.9 broadcast_multiply_fusion
  15.5 4.7 convolution_convert_fusion
  20.2 8.5 %collective-permute-done = bf16[4,256,1024]{2,1,0:T(8,128)(2,1)} collective-permute-done((bf16[4,256,1024]{2,1,0:T(8,128)(2,1)}, bf16[4,256,1024]{2,1,0:T(8,128)(2,1)}, u32[]{:S(2)}, u32[]{:S(2)}) %collective-permute-start) | collective-permute-done | bytes 2097184 | tf_op jit(solution)/shard_map/ppermute | solution.py:15
  28.7 4.4 collective-permute-done.1
  33.0 5.5 pad_maximum_fusion
  38.5 7.7 %gather_fusion = bf16[16,256,1024]{2,1,0:T(8,128)(2,1)} fusion(bf16[12,256,1024]{2,1,0:T(8,128)(2,1)} %pad_maximum_fusion, s32[1024]{0:T(1024)S(1)} %pad_clamp_fusion.2), kind=kCustom, calls=%fused_computation | custom fusion | bytes 16777280 | tf_op jit(solution)/shard_map/jit(_take)/gather | solution.py:48
  46.2 10.7 %fusion.9 = f32[16,200,200]{2,1,0:T(8,128)} fusion(bf16[16,200,1024]{2,1,0:T(8,128)(2,1)} %bitcast.17, bf16[16,256,200]{1,2,0:T(8,128)(2,1)S(1)} %copy-done.4, bf16[16,256,1024]{2,1,0:T(8,128)(2,1)} %gather_fusion, pred[16]{0:T(512)(128)(4,1)S(1)} %get-tuple-element.12), kind=kOutput, calls=%fused_computation.11 | convolution fusion | flops 2995912704 | bytes 19140624 | tf_op jit(solution)/shard_map/spk,sqk->spq/dot_general | solution.py:52
  56.9 4.0 collective-permute-start.2
  60.9 62.6 %collective-permute-done.2 = f32[16,200,200]{2,1,0:T(8,128)S(1)} collective-permute-done((f32[16,200,200]{2,1,0:T(8,128)}, f32[16,200,200]{2,1,0:T(8,128)S(1)}, u32[]{:S(2)}, u32[]{:S(2)}) %collective-permute-start.2) | collective-permute-done | bytes 2560032 | tf_op jit(solution)/shard_map/ppermute | solution.py:59
  123.5 2.3 add.62
  125.8 0.0 copy-start.5
  125.8 0.0 copy-start.1
  125.8 4.0 collective-permute-start.3
  129.9 265.0 %collective-permute-done.3 = f32[16,200,200]{2,1,0:T(8,128)S(1)} collective-permute-done((f32[16,200,200]{2,1,0:T(8,128)S(1)}, f32[16,200,200]{2,1,0:T(8,128)S(1)}, u32[]{:S(2)}, u32[]{:S(2)}) %collective-permute-start.3) | collective-permute-done | bytes 2560032 | tf_op jit(solution)/shard_map/ppermute | solution.py:59
  394.9 0.4 add.63
  395.3 1.9 collective-permute-start.4
  397.3 0.1 compare_select_fusion
  397.4 0.6 gather_fusion.1
  398.0 0.6 gather_fusion.2
  398.7 73.4 %collective-permute-done.4 = f32[16,200,200]{2,1,0:T(8,128)} collective-permute-done((f32[16,200,200]{2,1,0:T(8,128)S(1)}, f32[16,200,200]{2,1,0:T(8,128)}, u32[]{:S(2)}, u32[]{:S(2)}) %collective-permute-start.4) | collective-permute-done | bytes 2560032 | tf_op jit(solution)/shard_map/ppermute | solution.py:59
  472.1 1.8 dynamic-slice_add_fusion
  473.9 1.2 copy.14
  475.1 1.3 fusion.12
  476.4 0.9 copy.16
  477.3 0.1 fusion.16
  477.4 93.2 %psum.7 = f32[256]{0:T(256)S(1)} all-reduce(f32[256]{0:T(256)S(1)} %fusion.16), channel_id=1, replica_groups=mesh['occ'=64,'aux'=8] {'occ','aux'}, use_global_device_ids=true, to_apply=%region_2.3 | all-reduce | flops 256 | bytes 2048 | tf_op jit(solution)/shard_map/psum | solution.py:77
  570.7 0.6 dynamic_slice.19
  (16 shorter events, 0.1 us)
Async XLA Ops:
  0.6 398.0 %copy-start = (f32[16,200]{1,0:T(8,128)S(1)}, f32[16,200]{1,0:T(8,128)}, u32[]{:S(2)}) copy-start(f32[16,200]{1,0:T(8,128)} %param.8) | copy-start | bytes 38404
  0.6 14.8 %copy-start.2 = (bf16[4,256,1024]{2,1,0:T(8,128)(2,1)S(1)}, bf16[4,256,1024]{2,1,0:T(8,128)(2,1)}, u32[]{:S(2)}) copy-start(bf16[4,256,1024]{2,1,0:T(8,128)(2,1)} %param.6) | copy-start | bytes 6291460
  0.7 28.0 %collective-permute-start = (bf16[4,256,1024]{2,1,0:T(8,128)(2,1)}, bf16[4,256,1024]{2,1,0:T(8,128)(2,1)}, u32[]{:S(2)}, u32[]{:S(2)}) collective-permute-start(bf16[4,256,1024]{2,1,0:T(8,128)(2,1)} %param.6), channel_id=1, source_target_pairs={{0,8},{8,16},{16,24},{24,32},{32,40},{40,48},{48,56},{56,64},{64,7... | collective-permute-start | bytes 6291464 | tf_op jit(solution)/shard_map/ppermute | solution.py:15
  5.4 27.7 %collective-permute-start.1 = (bf16[4,256,1024]{2,1,0:T(8,128)(2,1)}, bf16[4,256,1024]{2,1,0:T(8,128)(2,1)}, u32[]{:S(2)}, u32[]{:S(2)}) collective-permute-start(bf16[4,256,1024]{2,1,0:T(8,128)(2,1)} %param.6), channel_id=1, source_target_pairs={{8,0},{16,8},{24,16},{32,24},{40,32},{48,40},{56,48},{64,56},{72,6... | collective-permute-start | bytes 6291464 | tf_op jit(solution)/shard_map/ppermute | solution.py:17
  15.5 4.7 copy-start.3
  38.5 7.7 %copy-start.4 = (bf16[16,256,200]{1,2,0:T(8,128)(2,1)S(1)}, bf16[16,256,200]{1,2,0:T(8,128)(2,1)}, u32[]{:S(2)}) copy-start(bf16[16,256,200]{1,2,0:T(8,128)(2,1)} %copy-done.3) | copy-start | bytes 4915204
  56.9 66.6 %collective-permute-start.2 = (f32[16,200,200]{2,1,0:T(8,128)}, f32[16,200,200]{2,1,0:T(8,128)S(1)}, u32[]{:S(2)}, u32[]{:S(2)}) collective-permute-start(f32[16,200,200]{2,1,0:T(8,128)} %fusion.9), channel_id=1, source_target_pairs={{0,1},{1,0},{2,3},{3,2},{4,5},{5,4},{6,7},{7,6},{8,9},{9,8},{10,11... | collective-permute-start | bytes 7680008 | tf_op jit(solution)/shard_map/ppermute | solution.py:59
  125.8 271.4 %copy-start.5 = (s32[16]{0:T(128)S(1)}, s32[16]{0:T(128)}, u32[]{:S(2)}) copy-start(s32[16]{0:T(128)} %param.10) | copy-start | bytes 196
  125.8 271.5 %copy-start.1 = (f32[256]{0:T(256)S(1)}, f32[256]{0:T(256)}, u32[]{:S(2)}) copy-start(f32[256]{0:T(256)} %param.9) | copy-start | bytes 3076
  125.8 269.0 %collective-permute-start.3 = (f32[16,200,200]{2,1,0:T(8,128)S(1)}, f32[16,200,200]{2,1,0:T(8,128)S(1)}, u32[]{:S(2)}, u32[]{:S(2)}) collective-permute-start(f32[16,200,200]{2,1,0:T(8,128)S(1)} %add.62), channel_id=1, source_target_pairs={{0,2},{1,3},{2,0},{3,1},{4,6},{5,7},{6,4},{7,5},{8,10},{9,11},{10,... | collective-permute-start | bytes 7680008 | tf_op jit(solution)/shard_map/ppermute | solution.py:59
  395.3 76.8 %collective-permute-start.4 = (f32[16,200,200]{2,1,0:T(8,128)S(1)}, f32[16,200,200]{2,1,0:T(8,128)}, u32[]{:S(2)}, u32[]{:S(2)}) collective-permute-start(f32[16,200,200]{2,1,0:T(8,128)S(1)} %add.63), channel_id=1, source_target_pairs={{0,4},{1,5},{2,6},{3,7},{4,0},{5,1},{6,2},{7,3},{8,12},{9,13},{10,... | collective-permute-start | bytes 7680008 | tf_op jit(solution)/shard_map/ppermute | solution.py:59
